TPU v7x, 256 devices: a whole 4x4x8 slice. The times are simulated.
256 devices in a mesh: gx: 4 (over x), gy: 8 (over z), gz: 8 (over y, core).
Axes of the slice: x: 4, y: 4, z: 8, core: 2. Of those that a mesh axis runs over, the one named last changes fastest.
Arguments:
- patch_fields: bfloat16 [8192, 4, 32768], P(('gx', 'gy', 'gz')), may hold values from -54 to 54
- slot_snapshot: int32 [8192], P(('gx', 'gy', 'gz')), may hold values from -1 to 15, as said below
- slot_brick: int32 [8192], P(('gx', 'gy', 'gz')), may hold values from -1 to 255, as said below
- prior_basis: float32 [64, 32], replicated, may hold values from -0.75 to 0.75
Outputs:
- gram_matrix: float32 [64, 64], replicated
- mode_fields: bfloat16 [64, 128, 4096], P('gx', 'gy', 'gz')
- diffused: bfloat16 [64, 128, 4096], P('gx', 'gy', 'gz')
- reduced: float32 [32, 32], replicated
Inputs may be any that keep to these rules, and one draw needn't show every extreme that they name: `slot_snapshot`: -1 marks an empty slot; on every device the live slots come first, and some device has all 32 slots live. `slot_brick`: a brick is named by its device index in the order gx, gy, gz with gz fastest; -1 exactly where slot_snapshot is -1; every pair of a snapshot and a brick is held by exactly one slot; a patch's owner has the same gz index as its brick; no device holds more than 1 patches of one brick, a bound reached in every gz plane.
All inputs are finite; a program needn't handle non-finite values.
Results may differ from a plain program's by a relative error of at most 0.0076.
Values may be sent and summed in bfloat16 or wider, within the bound.
A program may use at most 128 MiB of HBM per device.

v0:
```python
import jax
import jax.numpy as jnp
from jax import lax
from jax.sharding import Mesh
from jax.sharding import PartitionSpec as P

SNAPS = 16
FIELDS = 4
PATCH = 32
MODES = 32
EDGE = 16
CELLS = 4096
COLS = 64
GZ = ("gz_0", "gz_1")
GX_GY_GZ = ("gx", "gy", "gz_0", "gz_1")
HIGHEST = lax.Precision.HIGHEST


def extended(value, sides, width):
    edges = {}
    for axis, dim in sides:
        devices, length = (lax.axis_size(axis), value.shape[dim])
        up = [(i, (i + 1) % devices) for i in range(devices - 1)]
        last = lax.slice_in_dim(value, length - width, length, axis=dim)
        first = lax.slice_in_dim(value, 0, width, axis=dim)
        edges[dim] = (
            lax.ppermute(last, axis, up),
            lax.ppermute(first, axis, [(b, a) for a, b in up]),
        )
    done = []
    for _, dim in sides:
        low, high = edges[dim]
        around = [(width, width) if d in done else (0, 0) for d in range(value.ndim)]
        value = jnp.concatenate([jnp.pad(low, around), value, jnp.pad(high, around)], axis=dim)
        done.append(dim)
    return value


def extended_2(value, sides, width):
    for axis, dim in sides:
        devices, length = (lax.axis_size(axis), value.shape[dim])
        up = [(i, (i + 1) % devices) for i in range(devices - 1)]
        down = [(j, i) for i, j in up]
        last = lax.slice_in_dim(value, length - width, length, axis=dim)
        first = lax.slice_in_dim(value, 0, width, axis=dim)
        before = lax.ppermute(last, axis, up)
        after = lax.ppermute(first, axis, down)
        value = jnp.concatenate([before, value, after], axis=dim)
    return value


def over_axes(value, axes):
    for axis in axes:
        value = lax.psum(value, axis)
    return value


def average_cells(fine_data):
    row_count = fine_data.shape[0]
    view = fine_data.reshape(row_count * FIELDS * EDGE, 2, EDGE, 2 * PATCH)
    pair_x = view[:, 0].astype(jnp.float32) + view[:, 1].astype(jnp.float32)
    pair_y = pair_x[:, :, :PATCH] + pair_x[:, :, PATCH:]
    pairing = (
        jnp.arange(PATCH, dtype=jnp.int32)[:, None] // 2
        == jnp.arange(EDGE, dtype=jnp.int32)[None, :]
    ).astype(jnp.float32) * 0.125
    means = jnp.dot(pair_y.reshape(-1, PATCH), pairing, precision=HIGHEST)
    return means.reshape(row_count, FIELDS, CELLS).astype(jnp.bfloat16)


def seven_point(center, around_xy, around_z, stride):
    total = around_xy[2:, 1:-1] + around_xy[:-2, 1:-1] + around_xy[1:-1, 2:] + around_xy[1:-1, :-2]
    total = total + around_z[:, :, 2 * stride :] + around_z[:, :, : -2 * stride]
    return total - 6.0 * center


def factor_basis(gram_matrix, prior_basis):
    lower_factor = jnp.linalg.cholesky(gram_matrix)
    return lax.linalg.triangular_solve(
        lower_factor, prior_basis, left_side=True, lower=True, transpose_a=True
    )


def shards(patch_fields, slot_snapshot, slot_brick, prior_basis):
    size_x = lax.axis_size("gx")
    size_y = lax.axis_size("gy")
    size_z = lax.axis_size(GZ)
    plane_size = size_x * size_y
    slot_count = slot_snapshot.shape[0]
    pair_depth = slot_count // plane_size
    total_cells = CELLS * plane_size * size_z
    is_live = slot_snapshot >= 0
    slot_ids = jnp.arange(slot_count, dtype=jnp.int32)
    target_peer = jnp.where(is_live, slot_brick // size_z, plane_size)
    earlier = (target_peer[:, None] == target_peer[None, :]) & (
        slot_ids[None, :] < slot_ids[:, None]
    )
    pair_rank = jnp.sum(earlier.astype(jnp.int32), axis=1)
    position = jnp.where(is_live, target_peer * pair_depth + pair_rank, slot_count)
    slot_hits = position[:, None] == slot_ids[None, :]
    filled = jnp.any(slot_hits, axis=0)
    source = jnp.sum(jnp.where(slot_hits, slot_ids[:, None], 0), axis=0)
    sent_snapshot = jnp.where(filled, jnp.take(slot_snapshot, source), -1)
    payload = jnp.take(average_cells(patch_fields), source, axis=0)
    received, received_snapshot = (
        lax.all_to_all(payload, ("gx", "gy"), split_axis=0, concat_axis=0, tiled=True),
        lax.all_to_all(sent_snapshot, ("gx", "gy"), split_axis=0, concat_axis=0, tiled=True),
    )
    snapshots = jnp.arange(SNAPS, dtype=jnp.int32)
    chosen = jnp.sum(
        jnp.where(received_snapshot[None, :] == snapshots[:, None], slot_ids[None, :], 0), axis=1
    )
    arrived = jnp.take(received, chosen, axis=0)
    columns = arrived.reshape(COLS, CELLS)
    partial_gram = jnp.dot(columns, columns.T, preferred_element_type=jnp.float32)
    data_wide = columns.astype(jnp.float32).T
    data_block = columns.T.reshape(EDGE, EDGE, EDGE * COLS)
    data_xy = extended(data_block, (("gx", 0), ("gy", 1)), 1).astype(jnp.float32)
    data_z = extended_2(data_block, ((GZ, 2),), COLS).astype(jnp.float32)
    data_image = seven_point(data_block.astype(jnp.float32), data_xy, data_z, COLS).reshape(
        CELLS, COLS
    )
    partial_cross = jnp.dot(data_wide.T, data_image, precision=HIGHEST)
    gram_total, cross_total = (
        over_axes(partial_gram, GX_GY_GZ),
        over_axes(partial_cross, GX_GY_GZ),
    )
    gram_matrix = gram_total / total_cells
    coeffs = factor_basis(gram_matrix, prior_basis)
    mode_basis = jnp.dot(data_wide, coeffs, precision=HIGHEST)
    mode_image = jnp.dot(data_image, coeffs, precision=HIGHEST)
    inner = jnp.dot(cross_total / total_cells, coeffs, precision=HIGHEST)
    reduced = jnp.dot(coeffs.T, inner, precision=HIGHEST)
    mode_fields = mode_basis.reshape(EDGE, EDGE, EDGE * MODES).astype(jnp.bfloat16)
    diffused = mode_image.reshape(EDGE, EDGE, EDGE * MODES).astype(jnp.bfloat16)
    return (gram_matrix, mode_fields, diffused, reduced)


def solution(mesh):
    split = Mesh(
        mesh.devices.reshape(mesh.shape["gx"], mesh.shape["gy"], 4, 2), ("gx", "gy", "gz_0", "gz_1")
    )
    in_specs = (P(GX_GY_GZ, None, None), P(GX_GY_GZ), P(GX_GY_GZ), P())
    out_specs = (P(), P("gx", "gy", GZ), P("gx", "gy", GZ), P())
    return jax.shard_map(
        shards, mesh=split, in_specs=in_specs, out_specs=out_specs, check_vma=False
    )
```

profile of v0, /device:TPU:1, one launch (start us, length us, event | category | flops | bytes accessed | tf_op | source)
XLA Modules:
  0.0 251.8 jit_solution(11054224175543935289)
XLA Ops:
  4.4 11.9 %all-to-all-start = ((s32[32,1,1]{2,1,0:T(1,128)}), s32[32,1,1]{2,1,0:T(1,128)S(1)}, u32[]{:S(2)}, u32[]{:S(2)}) async-start(s32[32,1,1]{2,1,0:T(1,128)} %copy.36), calls=%async_computation | async-start | bytes 32768 | tf_op jit(solution)/shard_map/all_to_all | solution.py:107
  16.3 27.2 %reshape.237 = bf16[2048,2,16,64]{3,2,1,0:T(8,128)(2,1)} reshape(bf16[32,4,32768]{2,1,0:T(4,128)(2,1)} %param.4) | data formatting | bytes 16777216 | tf_op jit(solution)/shard_map/reshape | solution.py:60
  43.6 6.9 %add_bitcast_fusion = f32[2048,16,64]{2,1,0:T(8,128)S(1)} fusion(bf16[2048,2,16,64]{3,2,1,0:T(8,128)(2,1)} %reshape.237), kind=kLoop, calls=%fused_computation.5 | loop fusion | flops 6291456 | bytes 16777216 | tf_op jit(solution)/shard_map/add | solution.py:61
  50.5 7.5 %slice_add_fusion = f32[2048,16,32]{2,1,0:T(8,128)} fusion(f32[2048,16,64]{2,1,0:T(8,128)S(1)} %add_bitcast_fusion), kind=kLoop, calls=%fused_computation.4 | loop fusion | flops 1048576 | bytes 12582912 | tf_op jit(solution)/shard_map/add | solution.py:62
  58.0 17.3 %convolution_convert_fusion = bf16[32768,16]{0,1:T(8,128)(2,1)S(1)} fusion(f32[32768,32]{1,0:T(8,128)} %bitcast.40, s32[32]{0:T(128)S(1)} %and_select_fusion), kind=kOutput, calls=%fused_computation.3 | convolution fusion | flops 201851904 | bytes 5243008 | tf_op jit(solution)/shard_map/dot_general | solution.py:67
  75.3 6.2 %copy.37 = bf16[32768,16]{1,0:T(8,128)(2,1)} copy(bf16[32768,16]{0,1:T(8,128)(2,1)S(1)} %convolution_convert_fusion) | data formatting | bytes 2097152 | tf_op jit(solution)/shard_map/convert_element_type | solution.py:68
  81.5 10.8 %convert_element_type.47 = bf16[32,4,4096]{2,1,0:T(4,128)(2,1)S(1)} reshape(bf16[32768,16]{1,0:T(8,128)(2,1)} %copy.37) | data formatting | bytes 2097152 | tf_op jit(solution)/shard_map/convert_element_type | solution.py:68
  95.3 9.4 %all-to-all-start.1 = ((bf16[32,4,4096]{2,1,0:T(4,128)(2,1)}), bf16[32,4,4096]{2,1,0:T(4,128)(2,1)S(1)}, u32[]{:S(2)}, u32[]{:S(2)}) async-start(bf16[32,4,4096]{2,1,0:T(4,128)(2,1)} %broadcast_select_fusion), calls=%async_computation.1 | async-start | bytes 2097152 | tf_op jit(solution)/shard_map/all_to_all | solution.py:106
  105.7 23.5 %all-to-all-done.1 = bf16[32,4,4096]{2,1,0:T(4,128)(2,1)S(1)} async-done(((bf16[32,4,4096]{2,1,0:T(4,128)(2,1)}), bf16[32,4,4096]{2,1,0:T(4,128)(2,1)S(1)}, u32[]{:S(2)}, u32[]{:S(2)}) %all-to-all-start.1) | async-done | bytes 1048608 | tf_op jit(solution)/shard_map/all_to_all | solution.py:106
  132.1 8.2 %collective-permute-start.4 = (bf16[16,16,64]{2,1,0:T(8,128)(2,1)S(1)}, bf16[16,16,64]{2,1,0:T(8,128)(2,1)S(1)}, u32[]{:S(2)}, u32[]{:S(2)}) collective-permute-start(bf16[16,16,64]{2,1,0:T(8,128)(2,1)S(1)} %get-tuple-element.37), channel_id=1, source_target_pairs={{0,1},{1,2},{2,3},{3,4},{4,5},{5,6},{6,7},{8,9},{9,10},{10,11},{11... | collective-permute-start | bytes 98312 | tf_op jit(solution)/shard_map/ppermute | solution.py:46
  140.5 1.9 collective-permute-start.5
  143.7 4.0 %collective-permute-start = (bf16[16,1,1024]{2,1,0:T(2,128)(2,1)S(1)}, bf16[16,1,1024]{2,1,0:T(2,128)(2,1)S(1)}, u32[]{:S(2)}, u32[]{:S(2)}) collective-permute-start(bf16[16,1,1024]{2,1,0:T(2,128)(2,1)S(1)} %get-tuple-element.34), channel_id=1, source_target_pairs={{0,8},{8,16},{16,24},{24,32},{32,40},{40,48},{48,56},{1,9},{9,17},... | collective-permute-start | bytes 98312 | tf_op jit(solution)/shard_map/ppermute | solution.py:27
  149.2 4.0 %collective-permute-start.1 = (bf16[1,16,1024]{2,1,0:T(8,128)(2,1)S(1)}, bf16[1,16,1024]{2,1,0:T(8,128)(2,1)S(1)}, u32[]{:S(2)}, u32[]{:S(2)}) collective-permute-start(bf16[1,16,1024]{2,1,0:T(8,128)(2,1)S(1)} %slice.70), channel_id=1, source_target_pairs={{0,64},{64,128},{128,192},{1,65},{65,129},{129,193},{2,66},{66,130... | collective-permute-start | bytes 98312 | tf_op jit(solution)/shard_map/ppermute | solution.py:27
  157.8 1.8 fusion.31
  159.6 13.5 %all-reduce.4 = (f32[64,64]{0,1:T(8,128)S(1)}, f32[64,64]{0,1:T(8,128)S(1)}) all-reduce(f32[64,64]{0,1:T(8,128)S(1)} %fusion.30, f32[64,64]{0,1:T(8,128)S(1)} %fusion.31), channel_id=1, replica_groups=mesh['gx'=4,'gy'=8,'gz_0'=4,'gz_1'=2] {'gx'}, use_global_device_ids=true, to_apply=%region_4.5 | all-reduce | flops 8192 | bytes 65536 | tf_op jit(solution)/shard_map/psum | solution.py:54
  173.1 21.7 %all-reduce.2 = (f32[64,64]{0,1:T(8,128)S(1)}, f32[64,64]{0,1:T(8,128)S(1)}) all-reduce(f32[64,64]{0,1:T(8,128)S(1)} %get-tuple-element.28, f32[64,64]{0,1:T(8,128)S(1)} %get-tuple-element.29), channel_id=1, replica_groups=mesh['gx'=4,'gy'=8,'gz_0'=4,'gz_1'=2] {'gy'}, use_global_device_ids=true, to_apply=%region_5.6 | all-reduce | flops 8192 | bytes 65536 | tf_op jit(solution)/shard_map/psum | solution.py:54
  194.8 13.0 %all-reduce.3 = (f32[64,64]{0,1:T(8,128)S(1)}, f32[64,64]{0,1:T(8,128)S(1)}) all-reduce(f32[64,64]{0,1:T(8,128)S(1)} %get-tuple-element.24, f32[64,64]{0,1:T(8,128)S(1)} %get-tuple-element.25), channel_id=1, replica_groups=mesh['gx'=4,'gy'=8,'gz_0'=4,'gz_1'=2] {'gz_0'}, use_global_device_ids=true, to_apply=%region_6.7 | all-reduce | flops 8192 | bytes 65536 | tf_op jit(solution)/shard_map/psum | solution.py:54
  207.9 21.5 %all-reduce.5 = (f32[64,64]{0,1:T(8,128)S(1)}, f32[64,64]{0,1:T(8,128)S(1)}) all-reduce(f32[64,64]{0,1:T(8,128)S(1)} %get-tuple-element.26, f32[64,64]{0,1:T(8,128)S(1)} %get-tuple-element.27), channel_id=1, replica_groups=mesh['gx'=4,'gy'=8,'gz_0'=4,'gz_1'=2] {'gz_1'}, use_global_device_ids=true, to_apply=%region_7.8 | all-reduce | flops 8192 | bytes 65536 | tf_op jit(solution)/shard_map/psum | solution.py:54
  229.6 5.8 %cholesky.16 = f32[64,64]{1,0:T(8,128)S(1)} custom-call(f32[64,64]{1,0:T(8,128)S(1)} %fusion.11), custom_call_target="Cholesky" | custom-call | tf_op jit(solution)/shard_map/jit(cholesky)/cholesky | solution.py:78
  236.7 4.9 %custom-call.6 = f32[1,64,64]{1,2,0:T(8,128)S(1)} custom-call(f32[1,64,64]{2,1,0:T(8,128)S(1)} %fusion.8), custom_call_target="InvertDiagBlocksLowerTriangular" | custom-call | tf_op jit(solution)/shard_map/triangular_solve | solution.py:79
  241.8 2.4 convolution_convert_fusion.2
  244.2 2.3 convolution_convert_fusion.1
  247.0 1.7 convert_element_type.49
  249.2 1.7 convert_element_type.54
  (65 shorter events, 21.6 us)
Async XLA Ops:
  0.6 241.0 %copy-start = (f32[64,32]{0,1:T(8,128)S(1)}, f32[64,32]{0,1:T(8,128)}, u32[]{:S(2)}) copy-start(f32[64,32]{0,1:T(8,128)} %param.7) | copy-start | bytes 24580
  4.4 90.8 %all-to-all-start = ((s32[32,1,1]{2,1,0:T(1,128)}), s32[32,1,1]{2,1,0:T(1,128)S(1)}, u32[]{:S(2)}, u32[]{:S(2)}) async-start(s32[32,1,1]{2,1,0:T(1,128)} %copy.36), calls=%async_computation | async-start | bytes 32768 | tf_op jit(solution)/shard_map/all_to_all | solution.py:107
  95.3 33.9 %all-to-all-start.1 = ((bf16[32,4,4096]{2,1,0:T(4,128)(2,1)}), bf16[32,4,4096]{2,1,0:T(4,128)(2,1)S(1)}, u32[]{:S(2)}, u32[]{:S(2)}) async-start(bf16[32,4,4096]{2,1,0:T(4,128)(2,1)} %broadcast_select_fusion), calls=%async_computation.1 | async-start | bytes 2097152 | tf_op jit(solution)/shard_map/all_to_all | solution.py:106
  131.1 1.1 copy-start.1
  132.1 17.1 %collective-permute-start.4 = (bf16[16,16,64]{2,1,0:T(8,128)(2,1)S(1)}, bf16[16,16,64]{2,1,0:T(8,128)(2,1)S(1)}, u32[]{:S(2)}, u32[]{:S(2)}) collective-permute-start(bf16[16,16,64]{2,1,0:T(8,128)(2,1)S(1)} %get-tuple-element.37), channel_id=1, source_target_pairs={{0,1},{1,2},{2,3},{3,4},{4,5},{5,6},{6,7},{8,9},{9,10},{10,11},{11... | collective-permute-start | bytes 98312 | tf_op jit(solution)/shard_map/ppermute | solution.py:46
  140.5 13.1 %collective-permute-start.5 = (bf16[16,16,64]{2,1,0:T(8,128)(2,1)S(1)}, bf16[16,16,64]{2,1,0:T(8,128)(2,1)S(1)}, u32[]{:S(2)}, u32[]{:S(2)}) collective-permute-start(bf16[16,16,64]{2,1,0:T(8,128)(2,1)S(1)} %get-tuple-element.36), channel_id=1, source_target_pairs={{1,0},{2,1},{3,2},{4,3},{5,4},{6,5},{7,6},{9,8},{10,9},{11,10},{12... | collective-permute-start | bytes 98312 | tf_op jit(solution)/shard_map/ppermute | solution.py:47
  142.4 11.8 %collective-permute-start.3 = (bf16[16,1,1024]{2,1,0:T(2,128)(2,1)S(1)}, bf16[16,1,1024]{2,1,0:T(2,128)(2,1)S(1)}, u32[]{:S(2)}, u32[]{:S(2)}) collective-permute-start(bf16[16,1,1024]{2,1,0:T(2,128)(2,1)S(1)} %get-tuple-element.35), channel_id=1, source_target_pairs={{8,0},{16,8},{24,16},{32,24},{40,32},{48,40},{56,48},{9,1},{17,9},... | collective-permute-start | bytes 98312 | tf_op jit(solution)/shard_map/ppermute | solution.py:28
  143.7 10.6 %collective-permute-start = (bf16[16,1,1024]{2,1,0:T(2,128)(2,1)S(1)}, bf16[16,1,1024]{2,1,0:T(2,128)(2,1)S(1)}, u32[]{:S(2)}, u32[]{:S(2)}) collective-permute-start(bf16[16,1,1024]{2,1,0:T(2,128)(2,1)S(1)} %get-tuple-element.34), channel_id=1, source_target_pairs={{0,8},{8,16},{16,24},{24,32},{32,40},{40,48},{48,56},{1,9},{9,17},... | collective-permute-start | bytes 98312 | tf_op jit(solution)/shard_map/ppermute | solution.py:27
  147.8 6.5 %collective-permute-start.2 = (bf16[1,16,1024]{2,1,0:T(8,128)(2,1)S(1)}, bf16[1,16,1024]{2,1,0:T(8,128)(2,1)S(1)}, u32[]{:S(2)}, u32[]{:S(2)}) collective-permute-start(bf16[1,16,1024]{2,1,0:T(8,128)(2,1)S(1)} %slice.72), channel_id=1, source_target_pairs={{64,0},{128,64},{192,128},{65,1},{129,65},{193,129},{66,2},{130,66... | collective-permute-start | bytes 98312 | tf_op jit(solution)/shard_map/ppermute | solution.py:28
  149.2 5.0 %collective-permute-start.1 = (bf16[1,16,1024]{2,1,0:T(8,128)(2,1)S(1)}, bf16[1,16,1024]{2,1,0:T(8,128)(2,1)S(1)}, u32[]{:S(2)}, u32[]{:S(2)}) collective-permute-start(bf16[1,16,1024]{2,1,0:T(8,128)(2,1)S(1)} %slice.70), channel_id=1, source_target_pairs={{0,64},{64,128},{128,192},{1,65},{65,129},{129,193},{2,66},{66,130... | collective-permute-start | bytes 98312 | tf_op jit(solution)/shard_map/ppermute | solution.py:27
  229.5 16.9 %copy-start.2 = (f32[64,64]{1,0:T(8,128)}, f32[64,64]{1,0:T(8,128)S(1)}, u32[]{:S(2)}) copy-start(f32[64,64]{1,0:T(8,128)S(1)} %copy.44) | copy-start | bytes 49156
where the time goes:
time: 253 us; the launch traced here: 252 us
  blocking collectives  69.8 us (28%)
  local copies, waits for them, and re-layouts  57.5 us (23%)
  starting transfers between devices  42 us (17%)
  other arithmetic  32.9 us (13%)
  matrix products  25.1 us (10%)
  waiting for transfers between devices  23.5 us (9%)
    psum x4, blocking collectives, over_axes(): value = lax.psum(value, axis)  69.8 us
    reshape x1, local copies, waits for them, and re-layouts, average_cells(): view = fine_data.reshape(row_count * FIELDS * EDGE, 2, EDGE, 2 * PATCH)  27.2 us
    all_to_all x1, waiting for transfers between devices, shards(): lax.all_to_all(payload, ('gx', 'gy'), split_axis=0, concat_axis=0, tiled=...  23.5 us
    dot_general x1, matrix products, average_cells(): means = jnp.dot(pair_y.reshape(-1, PATCH), pairing, precision=HIGHEST)  17.3 us
    convert_element_type x2, local copies, waits for them, and re-layouts, average_cells(): return means.reshape(row_count, FIELDS, CELLS).astype(jnp.bfloat16)  17 us
    all_to_all x1, starting transfers between devices, shards(): lax.all_to_all(sent_snapshot, ('gx', 'gy'), split_axis=0, concat_axis=0,...  11.9 us
    all_to_all x1, starting transfers between devices, shards(): lax.all_to_all(payload, ('gx', 'gy'), split_axis=0, concat_axis=0, tiled=...  9.4 us
    ppermute x1, starting transfers between devices, extended_2(): before = lax.ppermute(last, axis, up)  8.21 us
  transfers between devices with their start and end apart: 8, of which 1 were waited for; matrix products, arithmetic and copies ran while one was open for 32% of the time, Pallas kernels for 0%

commit v1 on v0

--- a/solution.py
+++ b/solution.py
@@ -51,7 +51,8 @@
 
 def over_axes(value, axes):
     for axis in axes:
-        value = lax.psum(value, axis)
+        terms = lax.all_gather(value, axis, axis=0, tiled=False)
+        value = terms.sum(axis=0)
     return value
 
 

time: 253 us -> 284 us (1.12)
  blocking collectives: 69.8 us -> 108 us
  starting transfers between devices: 42 us -> 37.1 us
    all_gather x0 -> x8, blocking collectives: none -> 108 us  [over_axes(): terms = lax.all_gather(value, axis, axis=0, tiled=False)]
    psum x4 -> x0, blocking collectives: 69.8 us -> none  [over_axes(): value = lax.psum(value, axis)]
    ppermute x1, starting transfers between devices: 8.21 us -> 3.15 us  [extended_2(): before = lax.ppermute(last, axis, up)]
  transfers between devices with their start and end apart: 8 -> 8, of which waited for: 1 -> 1; matrix products, arithmetic and copies ran while one was open for 32% -> 30% of each run, Pallas kernels for 0% -> 0%
where the time goes in v1:
time: 284 us; the launch traced here: 283 us
  blocking collectives  108 us (38%)
  local copies, waits for them, and re-layouts  57.7 us (20%)
  starting transfers between devices  37.1 us (13%)
  other arithmetic  33 us (12%)
  waiting for transfers between devices  23.5 us (8%)
  matrix products  22.9 us (8%)
    all_gather x8, blocking collectives, over_axes(): terms = lax.all_gather(value, axis, axis=0, tiled=False)  108 us
    reshape x1, local copies, waits for them, and re-layouts, average_cells(): view = fine_data.reshape(row_count * FIELDS * EDGE, 2, EDGE, 2 * PATCH)  27.2 us
    all_to_all x1, waiting for transfers between devices, shards(): lax.all_to_all(payload, ('gx', 'gy'), split_axis=0, concat_axis=0, tiled=...  23.5 us
    dot_general x1, matrix products, average_cells(): means = jnp.dot(pair_y.reshape(-1, PATCH), pairing, precision=HIGHEST)  17.3 us
    convert_element_type x2, local copies, waits for them, and re-layouts, average_cells(): return means.reshape(row_count, FIELDS, CELLS).astype(jnp.bfloat16)  17 us
    all_to_all x1, starting transfers between devices, shards(): lax.all_to_all(sent_snapshot, ('gx', 'gy'), split_axis=0, concat_axis=0,...  11.9 us
    all_to_all x1, starting transfers between devices, shards(): lax.all_to_all(payload, ('gx', 'gy'), split_axis=0, concat_axis=0, tiled=...  9.4 us
    ppermute x2, starting transfers between devices, extended(): lax.ppermute(last, axis, up)  8.2 us
  transfers between devices with their start and end apart: 8, of which 1 were waited for; matrix products, arithmetic and copies ran while one was open for 30% of the time, Pallas kernels for 0%

profile of v1, /device:TPU:1, one launch (start us, length us, event | category | flops | bytes accessed | tf_op | source)
XLA Modules:
  0.0 282.9 jit_solution(12297041739814382499)
XLA Ops:
  4.4 11.9 %all-to-all-start = ((s32[32,1,1]{2,1,0:T(1,128)}), s32[32,1,1]{2,1,0:T(1,128)S(1)}, u32[]{:S(2)}, u32[]{:S(2)}) async-start(s32[32,1,1]{2,1,0:T(1,128)} %copy.30), calls=%async_computation | async-start | bytes 32768 | tf_op jit(solution)/shard_map/all_to_all | solution.py:108
  16.3 27.2 %reshape.237 = bf16[2048,2,16,64]{3,2,1,0:T(8,128)(2,1)} reshape(bf16[32,4,32768]{2,1,0:T(4,128)(2,1)} %param.4) | data formatting | bytes 16777216 | tf_op jit(solution)/shard_map/reshape | solution.py:61
  43.6 6.9 %add_bitcast_fusion = f32[2048,16,64]{2,1,0:T(8,128)S(1)} fusion(bf16[2048,2,16,64]{3,2,1,0:T(8,128)(2,1)} %reshape.237), kind=kLoop, calls=%fused_computation.5 | loop fusion | flops 6291456 | bytes 16777216 | tf_op jit(solution)/shard_map/add | solution.py:62
  50.5 7.5 %slice_add_fusion = f32[2048,16,32]{2,1,0:T(8,128)} fusion(f32[2048,16,64]{2,1,0:T(8,128)S(1)} %add_bitcast_fusion), kind=kLoop, calls=%fused_computation.4 | loop fusion | flops 1048576 | bytes 12582912 | tf_op jit(solution)/shard_map/add | solution.py:63
  58.0 17.3 %convolution_convert_fusion = bf16[32768,16]{0,1:T(8,128)(2,1)S(1)} fusion(f32[32768,32]{1,0:T(8,128)} %bitcast.48, s32[32]{0:T(128)S(1)} %and_select_fusion), kind=kOutput, calls=%fused_computation.3 | convolution fusion | flops 201851904 | bytes 5243008 | tf_op jit(solution)/shard_map/dot_general | solution.py:68
  75.3 6.2 %copy.31 = bf16[32768,16]{1,0:T(8,128)(2,1)} copy(bf16[32768,16]{0,1:T(8,128)(2,1)S(1)} %convolution_convert_fusion) | data formatting | bytes 2097152 | tf_op jit(solution)/shard_map/convert_element_type | solution.py:69
  81.5 10.8 %convert_element_type.47 = bf16[32,4,4096]{2,1,0:T(4,128)(2,1)S(1)} reshape(bf16[32768,16]{1,0:T(8,128)(2,1)} %copy.31) | data formatting | bytes 2097152 | tf_op jit(solution)/shard_map/convert_element_type | solution.py:69
  95.3 9.4 %all-to-all-start.1 = ((bf16[32,4,4096]{2,1,0:T(4,128)(2,1)}), bf16[32,4,4096]{2,1,0:T(4,128)(2,1)S(1)}, u32[]{:S(2)}, u32[]{:S(2)}) async-start(bf16[32,4,4096]{2,1,0:T(4,128)(2,1)} %broadcast_select_fusion), calls=%async_computation.1 | async-start | bytes 2097152 | tf_op jit(solution)/shard_map/all_to_all | solution.py:107
  105.7 23.5 %all-to-all-done.1 = bf16[32,4,4096]{2,1,0:T(4,128)(2,1)S(1)} async-done(((bf16[32,4,4096]{2,1,0:T(4,128)(2,1)}), bf16[32,4,4096]{2,1,0:T(4,128)(2,1)S(1)}, u32[]{:S(2)}, u32[]{:S(2)}) %all-to-all-start.1) | async-done | bytes 1048608 | tf_op jit(solution)/shard_map/all_to_all | solution.py:107
  132.6 9.1 %all-gather = f32[256,64]{1,0:T(8,128)S(1)} all-gather(f32[64,64]{1,0:T(8,128)S(1)} %fusion.30), channel_id=2, replica_groups=mesh['gx'=4,'gy'=8,'gz_0'=4,'gz_1'=2] {'gx'}, dimensions={0}, use_global_device_ids=true | all-gather | bytes 81920 | tf_op jit(solution)/shard_map/all_gather | solution.py:54
  141.7 19.7 %all-gather.1 = f32[512,64]{1,0:T(8,128)S(1)} all-gather(f32[64,64]{1,0:T(8,128)S(1)} %reduce_sum.111), channel_id=3, replica_groups=mesh['gx'=4,'gy'=8,'gz_0'=4,'gz_1'=2] {'gy'}, dimensions={0}, use_global_device_ids=true | all-gather | bytes 147456 | tf_op jit(solution)/shard_map/all_gather | solution.py:54
  161.4 9.9 %all-gather.2 = f32[256,64]{1,0:T(8,128)S(1)} all-gather(f32[64,64]{1,0:T(8,128)S(1)} %reduce_sum.112), channel_id=4, replica_groups=mesh['gx'=4,'gy'=8,'gz_0'=4,'gz_1'=2] {'gz_0'}, dimensions={0}, use_global_device_ids=true | all-gather | bytes 81920 | tf_op jit(solution)/shard_map/all_gather | solution.py:54
  171.4 17.3 %all-gather.3 = f32[128,64]{1,0:T(8,128)S(1)} all-gather(f32[64,64]{1,0:T(8,128)S(1)} %reduce_sum.113), channel_id=5, replica_groups=mesh['gx'=4,'gy'=8,'gz_0'=4,'gz_1'=2] {'gz_1'}, dimensions={0}, use_global_device_ids=true | all-gather | bytes 49152 | tf_op jit(solution)/shard_map/all_gather | solution.py:54
  188.9 5.8 %cholesky.16 = f32[64,64]{1,0:T(8,128)S(1)} custom-call(f32[64,64]{1,0:T(8,128)S(1)} %fusion.11), custom_call_target="Cholesky" | custom-call | tf_op jit(solution)/shard_map/jit(cholesky)/cholesky | solution.py:79
  196.1 4.9 %custom-call.6 = f32[1,64,64]{1,2,0:T(8,128)S(1)} custom-call(f32[1,64,64]{2,1,0:T(8,128)S(1)} %fusion.8), custom_call_target="InvertDiagBlocksLowerTriangular" | custom-call | tf_op jit(solution)/shard_map/triangular_solve | solution.py:80
  201.0 3.1 %collective-permute-start.4 = (bf16[16,16,64]{2,1,0:T(8,128)(2,1)S(1)}, bf16[16,16,64]{2,1,0:T(8,128)(2,1)S(1)}, u32[]{:S(2)}, u32[]{:S(2)}) collective-permute-start(bf16[16,16,64]{2,1,0:T(8,128)(2,1)S(1)} %get-tuple-element.29), channel_id=1, source_target_pairs={{0,1},{1,2},{2,3},{3,4},{4,5},{5,6},{6,7},{8,9},{9,10},{10,11},{11... | collective-permute-start | bytes 98312 | tf_op jit(solution)/shard_map/ppermute | solution.py:46
  204.1 1.9 collective-permute-start.5
  207.3 4.0 %collective-permute-start = (bf16[16,1,1024]{2,1,0:T(2,128)(2,1)S(1)}, bf16[16,1,1024]{2,1,0:T(2,128)(2,1)S(1)}, u32[]{:S(2)}, u32[]{:S(2)}) collective-permute-start(bf16[16,1,1024]{2,1,0:T(2,128)(2,1)S(1)} %get-tuple-element.26), channel_id=1, source_target_pairs={{0,8},{8,16},{16,24},{24,32},{32,40},{40,48},{48,56},{1,9},{9,17},... | collective-permute-start | bytes 98312 | tf_op jit(solution)/shard_map/ppermute | solution.py:27
  213.1 4.2 %collective-permute-start.1 = (bf16[1,16,1024]{2,1,0:T(8,128)(2,1)S(1)}, bf16[1,16,1024]{2,1,0:T(8,128)(2,1)S(1)}, u32[]{:S(2)}, u32[]{:S(2)}) collective-permute-start(bf16[1,16,1024]{2,1,0:T(8,128)(2,1)S(1)} %slice.70), channel_id=1, source_target_pairs={{0,64},{64,128},{128,192},{1,65},{65,129},{129,193},{2,66},{66,130... | collective-permute-start | bytes 98312 | tf_op jit(solution)/shard_map/ppermute | solution.py:27
  224.9 2.3 convolution_convert_fusion.1
  230.3 9.1 %all-gather.4 = f32[256,64]{1,0:T(8,128)S(1)} all-gather(f32[64,64]{1,0:T(8,128)S(1)} %fusion.31), channel_id=6, replica_groups=mesh['gx'=4,'gy'=8,'gz_0'=4,'gz_1'=2] {'gx'}, dimensions={0}, use_global_device_ids=true | all-gather | bytes 81920 | tf_op jit(solution)/shard_map/all_gather | solution.py:54
  239.4 18.4 %all-gather.5 = f32[512,64]{1,0:T(8,128)S(1)} all-gather(f32[64,64]{1,0:T(8,128)S(1)} %reduce_sum.115), channel_id=7, replica_groups=mesh['gx'=4,'gy'=8,'gz_0'=4,'gz_1'=2] {'gy'}, dimensions={0}, use_global_device_ids=true | all-gather | bytes 147456 | tf_op jit(solution)/shard_map/all_gather | solution.py:54
  257.8 9.1 %all-gather.6 = f32[256,64]{1,0:T(8,128)S(1)} all-gather(f32[64,64]{1,0:T(8,128)S(1)} %reduce_sum.116), channel_id=8, replica_groups=mesh['gx'=4,'gy'=8,'gz_0'=4,'gz_1'=2] {'gz_0'}, dimensions={0}, use_global_device_ids=true | all-gather | bytes 81920 | tf_op jit(solution)/shard_map/all_gather | solution.py:54
  267.0 15.0 %all-gather.7 = f32[128,64]{1,0:T(8,128)S(1)} all-gather(f32[64,64]{1,0:T(8,128)S(1)} %reduce_sum.117), channel_id=9, replica_groups=mesh['gx'=4,'gy'=8,'gz_0'=4,'gz_1'=2] {'gz_1'}, dimensions={0}, use_global_device_ids=true | all-gather | bytes 49152 | tf_op jit(solution)/shard_map/all_gather | solution.py:54
  (85 shorter events, 27.3 us)
Async XLA Ops:
  0.6 212.1 %copy-start = (f32[64,32]{0,1:T(8,128)S(1)}, f32[64,32]{0,1:T(8,128)}, u32[]{:S(2)}) copy-start(f32[64,32]{0,1:T(8,128)} %param.7) | copy-start | bytes 24580
  4.4 90.8 %all-to-all-start = ((s32[32,1,1]{2,1,0:T(1,128)}), s32[32,1,1]{2,1,0:T(1,128)S(1)}, u32[]{:S(2)}, u32[]{:S(2)}) async-start(s32[32,1,1]{2,1,0:T(1,128)} %copy.30), calls=%async_computation | async-start | bytes 32768 | tf_op jit(solution)/shard_map/all_to_all | solution.py:108
  95.3 33.9 %all-to-all-start.1 = ((bf16[32,4,4096]{2,1,0:T(4,128)(2,1)}), bf16[32,4,4096]{2,1,0:T(4,128)(2,1)S(1)}, u32[]{:S(2)}, u32[]{:S(2)}) async-start(bf16[32,4,4096]{2,1,0:T(4,128)(2,1)} %broadcast_select_fusion), calls=%async_computation.1 | async-start | bytes 2097152 | tf_op jit(solution)/shard_map/all_to_all | solution.py:107
  105.6 25.4 %copy-start.4 = (pred[64]{0:T(512)(128)(4,1)}, pred[64]{0:T(512)(128)(4,1)S(1)}, u32[]{:S(2)}) copy-start(pred[64]{0:T(512)(128)(4,1)S(1)} %broadcast_in_dim.95) | copy-start | bytes 196
  131.1 1.1 copy-start.1
  132.2 85.1 %copy-start.2 = (bf16[64,4096]{0,1:T(8,128)(2,1)S(1)}, bf16[64,4096]{0,1:T(8,128)(2,1)}, u32[]{:S(2)}) copy-start(bf16[64,4096]{0,1:T(8,128)(2,1)} %copy-done.1) | copy-start | bytes 1572868
  132.2 85.1 %copy-start.5 = (pred[64]{0:T(512)(128)(4,1)S(1)}, pred[64]{0:T(512)(128)(4,1)}, u32[]{:S(2)}) copy-start(pred[64]{0:T(512)(128)(4,1)} %copy-done.4) | copy-start | bytes 196
  188.8 31.8 %copy-start.3 = (f32[64,64]{1,0:T(8,128)}, f32[64,64]{1,0:T(8,128)S(1)}, u32[]{:S(2)}) copy-start(f32[64,64]{1,0:T(8,128)S(1)} %copy.38) | copy-start | bytes 49156
  201.0 12.1 %collective-permute-start.4 = (bf16[16,16,64]{2,1,0:T(8,128)(2,1)S(1)}, bf16[16,16,64]{2,1,0:T(8,128)(2,1)S(1)}, u32[]{:S(2)}, u32[]{:S(2)}) collective-permute-start(bf16[16,16,64]{2,1,0:T(8,128)(2,1)S(1)} %get-tuple-element.29), channel_id=1, source_target_pairs={{0,1},{1,2},{2,3},{3,4},{4,5},{5,6},{6,7},{8,9},{9,10},{10,11},{11... | collective-permute-start | bytes 98312 | tf_op jit(solution)/shard_map/ppermute | solution.py:46
  204.1 16.5 %collective-permute-start.5 = (bf16[16,16,64]{2,1,0:T(8,128)(2,1)S(1)}, bf16[16,16,64]{2,1,0:T(8,128)(2,1)S(1)}, u32[]{:S(2)}, u32[]{:S(2)}) collective-permute-start(bf16[16,16,64]{2,1,0:T(8,128)(2,1)S(1)} %get-tuple-element.28), channel_id=1, source_target_pairs={{1,0},{2,1},{3,2},{4,3},{5,4},{6,5},{7,6},{9,8},{10,9},{11,10},{12... | collective-permute-start | bytes 98312 | tf_op jit(solution)/shard_map/ppermute | solution.py:47
  206.0 15.3 %collective-permute-start.3 = (bf16[16,1,1024]{2,1,0:T(2,128)(2,1)S(1)}, bf16[16,1,1024]{2,1,0:T(2,128)(2,1)S(1)}, u32[]{:S(2)}, u32[]{:S(2)}) collective-permute-start(bf16[16,1,1024]{2,1,0:T(2,128)(2,1)S(1)} %get-tuple-element.27), channel_id=1, source_target_pairs={{8,0},{16,8},{24,16},{32,24},{40,32},{48,40},{56,48},{9,1},{17,9},... | collective-permute-start | bytes 98312 | tf_op jit(solution)/shard_map/ppermute | solution.py:28
  207.3 14.0 %collective-permute-start = (bf16[16,1,1024]{2,1,0:T(2,128)(2,1)S(1)}, bf16[16,1,1024]{2,1,0:T(2,128)(2,1)S(1)}, u32[]{:S(2)}, u32[]{:S(2)}) collective-permute-start(bf16[16,1,1024]{2,1,0:T(2,128)(2,1)S(1)} %get-tuple-element.26), channel_id=1, source_target_pairs={{0,8},{8,16},{16,24},{24,32},{32,40},{40,48},{48,56},{1,9},{9,17},... | collective-permute-start | bytes 98312 | tf_op jit(solution)/shard_map/ppermute | solution.py:27
  211.5 9.9 %collective-permute-start.2 = (bf16[1,16,1024]{2,1,0:T(8,128)(2,1)S(1)}, bf16[1,16,1024]{2,1,0:T(8,128)(2,1)S(1)}, u32[]{:S(2)}, u32[]{:S(2)}) collective-permute-start(bf16[1,16,1024]{2,1,0:T(8,128)(2,1)S(1)} %slice.72), channel_id=1, source_target_pairs={{64,0},{128,64},{192,128},{65,1},{129,65},{193,129},{66,2},{130,66... | collective-permute-start | bytes 98312 | tf_op jit(solution)/shard_map/ppermute | solution.py:28
  213.1 8.3 %collective-permute-start.1 = (bf16[1,16,1024]{2,1,0:T(8,128)(2,1)S(1)}, bf16[1,16,1024]{2,1,0:T(8,128)(2,1)S(1)}, u32[]{:S(2)}, u32[]{:S(2)}) collective-permute-start(bf16[1,16,1024]{2,1,0:T(8,128)(2,1)S(1)} %slice.70), channel_id=1, source_target_pairs={{0,64},{64,128},{128,192},{1,65},{65,129},{129,193},{2,66},{66,130... | collective-permute-start | bytes 98312 | tf_op jit(solution)/shard_map/ppermute | solution.py:27
